TPU v7x, 512 devices: a whole 4x4x16 slice. The times are simulated.
512 devices in a mesh: row: 32 (over z, core), col: 16 (over x, y).
Axes of the slice: x: 4, y: 4, z: 16, core: 2. Of those that a mesh axis runs over, the one named last changes fastest.
Arguments:
- x_points: bfloat16 [131072, 256], P(('row', 'col')), may hold values from -1.5 to 1.5
- y_points: bfloat16 [131072, 256], P(('row', 'col')), may hold values from -1.5 to 1.5
- log_a: float32 [131072], P(('row', 'col')), may hold values from -1.5 to 1.5
- log_b: float32 [131072], P(('row', 'col')), may hold values from -1.5 to 1.5
- g_init: float32 [131072], P(('row', 'col')), may hold values from -3 to 3
- tile_list: int32 [24576, 2], P(('row', 'col')), may hold values from 0 to 1023, as said below
- tile_count: int32 [512], P(('row', 'col')), may hold values from 2 to 48, as said below
Outputs:
- f_out: float32 [131072], P(('row', 'col'))
- g_out: float32 [131072], P(('row', 'col'))
Inputs may be any that keep to these rules, and one draw needn't show every extreme that they name: `tile_list`: slots 48 * d to 48 * (d + 1) - 1 belong to device d = row index * 16 + col index. Each slot names a source block held by a device of d's row group and a target block held by a device of d's col group; the slots of one device are distinct pairs. Every block of either cloud is in some active tile. `tile_count`: some device has all 48 slots active.
All inputs are finite; a program needn't handle non-finite values.
Results may differ from a plain program's by a relative error of at most 0.0003.
Values may be sent and summed in bfloat16 or wider, within the bound.
A program may use at most 64 MiB of HBM per device.

v0:
```python
import math
import jax
import jax.numpy as jnp
from jax import lax
from jax.sharding import PartitionSpec as P

BLOCK = 128
ITERS = 2
EPSILON = 0.25
NEGATIVE = -1e30


def block_costs(x_blocks, x_square, y_blocks, y_square, rows, cols):
    x_take = jnp.take(x_blocks, rows, axis=0)
    y_take = jnp.take(y_blocks, cols, axis=0)
    inner = jnp.einsum("tpd,tqd->tpq", x_take, y_take, preferred_element_type=jnp.float32)
    return (
        0.5 * jnp.take(x_square, rows, axis=0)[:, :, None]
        + 0.5 * jnp.take(y_square, cols, axis=0)[:, None, :]
        - inner
    )


def local_max(score_of, targets, shape_blocks, turns):

    def visit(turn_index, acc):
        return acc.at[targets[turn_index]].max(jnp.max(score_of(turn_index), axis=-1))

    return lax.fori_loop(0, turns, visit, jnp.full(shape_blocks, NEGATIVE, jnp.float32))


def local_sum(score_of, targets, top, turns):

    def visit(turn_index, acc):
        rows = targets[turn_index]
        shift = jnp.take(top, rows, axis=0)[:, :, None]
        return acc.at[rows].add(jnp.sum(jnp.exp(score_of(turn_index) - shift), axis=-1))

    return lax.fori_loop(0, turns, visit, jnp.zeros(top.shape, jnp.float32))


def row_potential(score_of, targets, shape_blocks, turns):
    top = lax.pmax(local_max(score_of, targets, shape_blocks, turns), "col")
    total = lax.psum(local_sum(score_of, targets, top, turns), "col")
    return -EPSILON * (top + jnp.log(total))


def col_potential(score_of, targets, shape_blocks, turns):
    top = lax.pmax(
        local_max(score_of, targets, shape_blocks, turns).astype(jnp.bfloat16), "row"
    ).astype(jnp.float32)
    total = lax.psum(local_sum(score_of, targets, top, turns), "row")
    return -EPSILON * (top + jnp.log(total))


def body(x_points, y_points, log_a, log_b, g_init, tile_list, tile_count):
    width = x_points.shape[1]
    points_here = x_points.shape[0]
    per_device = points_here // BLOCK
    row_index = lax.axis_index("row")
    col_index = lax.axis_index("col")
    col_count = lax.axis_size("col")
    x_all = lax.all_gather(x_points, "col", axis=0, tiled=True)
    a_all = lax.all_gather(log_a, "col", axis=0, tiled=True)
    y_all = lax.all_gather(y_points, "row", axis=0, tiled=True)
    y_extra = lax.all_gather(jnp.stack([log_b, g_init]), "row", axis=1, tiled=True)
    x_blocks = x_all.reshape(-1, BLOCK, width)
    y_blocks = y_all.reshape(-1, BLOCK, width)
    x_square = jnp.einsum("bpd,bpd->bp", x_blocks, x_blocks, preferred_element_type=jnp.float32)
    y_square = jnp.einsum("bpd,bpd->bp", y_blocks, y_blocks, preferred_element_type=jnp.float32)
    a_blocks = a_all.reshape(-1, BLOCK)
    b_blocks = y_extra[0].reshape(-1, BLOCK)
    g_blocks = y_extra[1].reshape(-1, BLOCK)
    tiles_here = tile_list.shape[0]
    batch = math.gcd(tiles_here, 8)
    turns = tiles_here // batch
    row_ids = (tile_list[:, 0] - row_index * (col_count * per_device)).reshape(turns, batch)
    col_global = tile_list[:, 1]
    col_ids = (
        col_global // per_device // col_count * per_device + col_global % per_device
    ).reshape(turns, batch)
    active = (jnp.arange(tiles_here, dtype=jnp.int32) < tile_count[0]).reshape(turns, batch)

    def costs_at(turn_index):
        return block_costs(
            x_blocks, x_square, y_blocks, y_square, row_ids[turn_index], col_ids[turn_index]
        )

    f_blocks = jnp.zeros_like(a_blocks)
    for iteration in range(ITERS):

        def f_scores(turn_index):
            cols = col_ids[turn_index]
            scores = (
                jnp.take(g_blocks, cols, axis=0)[:, None, :] - costs_at(turn_index)
            ) / EPSILON + jnp.take(b_blocks, cols, axis=0)[:, None, :]
            return jnp.where(active[turn_index][:, None, None], scores, NEGATIVE)

        f_blocks = row_potential(f_scores, row_ids, a_blocks.shape, turns)

        def g_scores(turn_index):
            rows = row_ids[turn_index]
            scores = (
                jnp.take(f_blocks, rows, axis=0)[:, :, None] - costs_at(turn_index)
            ) / EPSILON + jnp.take(a_blocks, rows, axis=0)[:, :, None]
            scores = jnp.transpose(scores, (0, 2, 1))
            return jnp.where(active[turn_index][:, None, None], scores, NEGATIVE)

        g_blocks = col_potential(g_scores, col_ids, b_blocks.shape, turns)
    f_out = lax.dynamic_slice_in_dim(f_blocks.reshape(-1), col_index * points_here, points_here)
    g_out = lax.dynamic_slice_in_dim(g_blocks.reshape(-1), row_index * points_here, points_here)
    return (f_out, g_out)


def solution(mesh):
    in_specs = (
        P(("row", "col"), None),
        P(("row", "col"), None),
        P(("row", "col")),
        P(("row", "col")),
        P(("row", "col")),
        P(("row", "col"), None),
        P(("row", "col")),
    )
    out_specs = (P(("row", "col")), P(("row", "col")))
    return jax.shard_map(body, mesh=mesh, in_specs=in_specs, out_specs=out_specs, check_vma=False)
```

profile of v0, /device:TPU:1, one launch (start us, length us, event | category | flops | bytes accessed | tf_op | source)
XLA Modules:
  0.0 1156.1 jit_solution(3154675278406226549)
XLA Ops:
  10.2 19.6 %all-gather = f32[16,1,256]{2,1,0:T(1,128)S(1)} all-gather(f32[1,1,256]{2,1,0:T(1,128)} %bitcast.181), channel_id=1, replica_groups=mesh['row'=32,'col'=16] {'col'}, dimensions={0}, use_global_device_ids=true | all-gather | bytes 17408 | tf_op jit(solution)/shard_map/all_gather | solution.py:64
  30.5 41.8 %all_gather.12 = f32[2,8192]{1,0:T(2,128)S(1)} all-gather(f32[2,256]{1,0:T(2,128)S(1)} %pad_maximum_fusion), channel_id=1, replica_groups=mesh['row'=32,'col'=16] {'row'}, dimensions={1}, use_global_device_ids=true | all-gather | bytes 67584 | tf_op jit(solution)/shard_map/all_gather | solution.py:66
  77.3 74.6 %all-gather.6.cloned.1.call-done = bf16[8192,256]{1,0:T(8,128)(2,1)} async-done(((bf16[256,256]{1,0:T(8,128)(2,1)}), bf16[8192,256]{1,0:T(8,128)(2,1)}) %all-gather.6.cloned.1.call-update) | async-done | bytes 4194320 | tf_op jit(solution)/shard_map/all_gather | solution.py:65
  151.9 3.3 fusion.112
  155.2 42.2 %while.104 = (s32[]{:T(128)}, f32[32,128]{1,0:T(8,128)S(1)}, s32[6,8]{1,0:T(8,128)S(1)}, pred[6,8]{1,0:T(8,128)(4,1)S(1)}, s32[6,8]{1,0:T(8,128)S(1)}, /*index=5...) while((s32[]{:T(128)}, f32[32,128]{1,0:T(8,128)S(1)}, ...), condition=%wide.region_3.8_spmd, body=%wide.region_0.7_spmd.sunk | while | flops 68558968 | bytes 3252905 | solution.py:29
  197.5 60.4 %pmax.28 = f32[32,128]{1,0:T(8,128)S(1)} all-reduce(f32[32,128]{1,0:T(8,128)S(1)} %get-tuple-element.1538), channel_id=1, replica_groups=mesh['row'=32,'col'=16] {'col'}, use_global_device_ids=true, to_apply=%region_4.9 | all-reduce | flops 4096 | bytes 32768 | tf_op jit(solution)/shard_map/pmax | solution.py:43
  257.9 45.7 %while.105 = (s32[]{:T(128)}, f32[32,128]{1,0:T(8,128)S(1)}, s32[6,8]{1,0:T(8,128)S(1)}, pred[6,8]{1,0:T(8,128)(4,1)S(1)}, s32[6,8]{1,0:T(8,128)S(1)}, /*index=5...) while((s32[]{:T(128)}, f32[32,128]{1,0:T(8,128)S(1)}, ...), condition=%wide.region_8.13_spmd, body=%wide.region_5.12_spmd.sunk | while | flops 68691064 | bytes 3273425 | solution.py:39
  303.6 56.0 %psum.28 = f32[32,128]{1,0:T(8,128)S(1)} all-reduce(f32[32,128]{1,0:T(8,128)S(1)} %get-tuple-element.1539), channel_id=1, replica_groups=mesh['row'=32,'col'=16] {'col'}, use_global_device_ids=true, to_apply=%region_9.14 | all-reduce | flops 4096 | bytes 32768 | tf_op jit(solution)/shard_map/psum | solution.py:44
  359.6 42.5 %while.106 = (s32[]{:T(128)}, f32[64,128]{1,0:T(8,128)S(1)}, s32[6,8]{1,0:T(8,128)S(1)}, pred[6,8]{1,0:T(8,128)(4,1)S(1)}, s32[6,8]{1,0:T(8,128)S(1)}, /*index=5...) while((s32[]{:T(128)}, f32[64,128]{1,0:T(8,128)S(1)}, ...), condition=%wide.region_13.18_spmd, body=%wide.region_10.17_spmd.sunk | while | flops 68558968 | bytes 3252905 | solution.py:29
  362.6 2.8 gather_fusion.14
  369.7 2.8 gather_fusion.14
  391.0 2.8 gather_fusion.14
  398.1 2.8 gather_fusion.14
  402.2 114.2 %pmax.29 = bf16[64,128]{1,0:T(8,128)(2,1)S(1)} all-reduce(bf16[64,128]{1,0:T(8,128)(2,1)S(1)} %convert_element_type.12), channel_id=1, replica_groups=mesh['row'=32,'col'=16] {'row'}, use_global_device_ids=true, to_apply=%region_14.19 | all-reduce | flops 8192 | bytes 32768 | tf_op jit(solution)/shard_map/pmax | solution.py:49
  516.4 45.9 %while.107 = (s32[]{:T(128)}, f32[64,128]{1,0:T(8,128)S(1)}, s32[6,8]{1,0:T(8,128)S(1)}, pred[6,8]{1,0:T(8,128)(4,1)S(1)}, s32[6,8]{1,0:T(8,128)S(1)}, /*index=5...) while((s32[]{:T(128)}, f32[64,128]{1,0:T(8,128)S(1)}, ...), condition=%wide.region_18.23_spmd, body=%wide.region_15.22_spmd.sunk | while | flops 68691064 | bytes 3273425 | solution.py:39
  519.9 2.8 gather_fusion.20
  535.3 2.8 gather_fusion.20
  542.9 2.8 gather_fusion.20
  550.6 2.8 gather_fusion.20
  558.2 2.8 gather_fusion.20
  562.3 90.0 %psum.29 = f32[64,128]{1,0:T(8,128)S(1)} all-reduce(f32[64,128]{1,0:T(8,128)S(1)} %get-tuple-element.1541), channel_id=1, replica_groups=mesh['row'=32,'col'=16] {'row'}, use_global_device_ids=true, to_apply=%region_19.24 | all-reduce | flops 8192 | bytes 65536 | tf_op jit(solution)/shard_map/psum | solution.py:52
  652.3 42.2 %while.108 = (s32[]{:T(128)}, f32[32,128]{1,0:T(8,128)S(1)}, s32[6,8]{1,0:T(8,128)S(1)}, pred[6,8]{1,0:T(8,128)(4,1)S(1)}, s32[6,8]{1,0:T(8,128)S(1)}, /*index=5...) while((s32[]{:T(128)}, f32[32,128]{1,0:T(8,128)S(1)}, ...), condition=%wide.region_23.28_spmd, body=%wide.region_20.27_spmd.sunk | while | flops 68558968 | bytes 3252905 | solution.py:29
  694.6 55.7 %pmax.30 = f32[32,128]{1,0:T(8,128)S(1)} all-reduce(f32[32,128]{1,0:T(8,128)S(1)} %get-tuple-element.1542), channel_id=1, replica_groups=mesh['row'=32,'col'=16] {'col'}, use_global_device_ids=true, to_apply=%region_24.29 | all-reduce | flops 4096 | bytes 32768 | tf_op jit(solution)/shard_map/pmax | solution.py:43
  750.3 45.7 %while.109 = (s32[]{:T(128)}, f32[32,128]{1,0:T(8,128)S(1)}, s32[6,8]{1,0:T(8,128)S(1)}, pred[6,8]{1,0:T(8,128)(4,1)S(1)}, s32[6,8]{1,0:T(8,128)S(1)}, /*index=5...) while((s32[]{:T(128)}, f32[32,128]{1,0:T(8,128)S(1)}, ...), condition=%wide.region_28.33_spmd, body=%wide.region_25.32_spmd.sunk | while | flops 68691064 | bytes 3273425 | solution.py:39
  795.9 56.0 %psum.30 = f32[32,128]{1,0:T(8,128)S(1)} all-reduce(f32[32,128]{1,0:T(8,128)S(1)} %get-tuple-element.1543), channel_id=1, replica_groups=mesh['row'=32,'col'=16] {'col'}, use_global_device_ids=true, to_apply=%region_29.34 | all-reduce | flops 4096 | bytes 32768 | tf_op jit(solution)/shard_map/psum | solution.py:44
  851.9 42.5 %while.110 = (s32[]{:T(128)}, f32[64,128]{1,0:T(8,128)S(1)}, s32[6,8]{1,0:T(8,128)S(1)}, pred[6,8]{1,0:T(8,128)(4,1)S(1)}, s32[6,8]{1,0:T(8,128)S(1)}, /*index=5...) while((s32[]{:T(128)}, f32[64,128]{1,0:T(8,128)S(1)}, ...), condition=%wide.region_33.38_spmd, body=%wide.region_30.37_spmd.sunk | while | flops 68558968 | bytes 3252905 | solution.py:29
  855.0 2.8 gather_fusion.40
  862.0 2.8 gather_fusion.40
  869.1 2.8 gather_fusion.40
  894.5 117.5 %pmax.31 = bf16[64,128]{1,0:T(8,128)(2,1)S(1)} all-reduce(bf16[64,128]{1,0:T(8,128)(2,1)S(1)} %convert_element_type.14), channel_id=1, replica_groups=mesh['row'=32,'col'=16] {'row'}, use_global_device_ids=true, to_apply=%region_34.39 | all-reduce | flops 8192 | bytes 32768 | tf_op jit(solution)/shard_map/pmax | solution.py:49
  1012.0 45.9 %while.111 = (s32[]{:T(128)}, f32[64,128]{1,0:T(8,128)S(1)}, s32[6,8]{1,0:T(8,128)S(1)}, pred[6,8]{1,0:T(8,128)(4,1)S(1)}, s32[6,8]{1,0:T(8,128)S(1)}, /*index=5...) while((s32[]{:T(128)}, f32[64,128]{1,0:T(8,128)S(1)}, ...), condition=%wide.region_38.43_spmd, body=%wide.region_35.42_spmd.sunk | while | flops 68691064 | bytes 3273425 | solution.py:39
  1057.9 90.0 %psum.31 = f32[64,128]{1,0:T(8,128)S(1)} all-reduce(f32[64,128]{1,0:T(8,128)S(1)} %get-tuple-element.1545), channel_id=1, replica_groups=mesh['row'=32,'col'=16] {'row'}, use_global_device_ids=true, to_apply=%region_39.44 | all-reduce | flops 8192 | bytes 65536 | tf_op jit(solution)/shard_map/psum | solution.py:52
  (765 shorter events, 324.8 us)
Async XLA Ops:
  7.2 67.8 %all-gather.4.cloned.1.call-start = ((), (), s32[]{:S(2)}) async-start(), calls=%async_computation | async-start | bytes 2228224 | tf_op jit(solution)/shard_map/all_gather | solution.py:63
  7.9 144.0 %all-gather.6.cloned.1.call-start = ((), (), s32[]{:S(2)}) async-start(), calls=%async_computation.1 | async-start | bytes 4325376 | tf_op jit(solution)/shard_map/all_gather | solution.py:65
  75.0 80.3 %copy-start = (bf16[4096,256]{1,0:T(8,128)(2,1)S(1)}, bf16[4096,256]{1,0:T(8,128)(2,1)}, u32[]{:S(2)}) copy-start(bf16[4096,256]{1,0:T(8,128)(2,1)} %all-gather.4.cloned.1.call-done) | copy-start | bytes 6291460
Sparse Core Ops, SparseCore 0:
  11.0 63.9 all-gather.3
  77.1 74.7 all-gather.5
where the time goes:
time: 1160 us
  blocking collectives  701 us (60%)
  local copies, waits for them, and re-layouts  283 us (24%)
  waiting for transfers between devices  78.4 us (7%)
  other arithmetic  47.9 us (4%)
  matrix products  26.8 us (2%)
  between operations  14.9 us (1%)
    pmax x2, blocking collectives, col_potential(): lax.pmax(local_max(score_of, targets, shape_blocks, turns).astype(jnp.bfl...  232 us
    psum x2, blocking collectives, col_potential(): total = lax.psum(local_sum(score_of, targets, top, turns), 'row')  180 us
    gather x48, local copies, waits for them, and re-layouts, block_costs(): y_take = jnp.take(y_blocks, cols, axis=0)  133 us
    pmax x2, blocking collectives, row_potential(): top = lax.pmax(local_max(score_of, targets, shape_blocks, turns), 'col')  116 us
    psum x2, blocking collectives, row_potential(): total = lax.psum(local_sum(score_of, targets, top, turns), 'col')  112 us
    all_gather x1, waiting for transfers between devices, body(): y_all = lax.all_gather(y_points, 'row', axis=0, tiled=True)  74.6 us
    all_gather x1, blocking collectives, body(): lax.all_gather(jnp.stack([log_b, g_init]), 'row', axis=1, tiled=True)  41.8 us
    gather x48, local copies, waits for them, and re-layouts, block_costs(): x_take = jnp.take(x_blocks, rows, axis=0)  27.8 us
  transfers between devices with their start and end apart: 2, of which 2 were waited for; matrix products, arithmetic and copies ran while one was open for 0% of the time, Pallas kernels for 0%

commit v1 on v0

--- a/solution.py
+++ b/solution.py
@@ -40,8 +40,14 @@
 
 
 def row_potential(score_of, targets, shape_blocks, turns):
+
+    def _do_matrix(work_x, axis_key):
+        back = lax.all_gather(work_x, axis_name=axis_key)
+        mat_out = jnp.sum(back, 0)
+        return mat_out
+
     top = lax.pmax(local_max(score_of, targets, shape_blocks, turns), "col")
-    total = lax.psum(local_sum(score_of, targets, top, turns), "col")
+    total = _do_matrix(local_sum(score_of, targets, top, turns), "col")
     return -EPSILON * (top + jnp.log(total))
 
 

time: 1160 us -> 1070 us (0.922)
  blocking collectives: 701 us -> 606 us
    psum x2 -> x0, blocking collectives: 112 us -> none  [row_potential(): total = lax.psum(local_sum(score_of, targets, top, turns), 'col')]
    all_gather x0 -> x2, blocking collectives: none -> 31 us  [_do_matrix(): back = lax.all_gather(work_x, axis_name=axis_key)]
    pmax x2, blocking collectives: 232 us -> 215 us  [col_potential(): lax.pmax(local_max(score_of, targets, shape_blocks, turns).astype(jnp.bfl...]
where the time goes in v1:
time: 1070 us; the launch traced here: 1060 us
  blocking collectives  606 us (57%)
  local copies, waits for them, and re-layouts  283 us (26%)
  waiting for transfers between devices  78.4 us (7%)
  other arithmetic  48 us (4%)
  matrix products  26.8 us (3%)
  between operations  14.9 us (1%)
    pmax x2, blocking collectives, col_potential(): lax.pmax(local_max(score_of, targets, shape_blocks, turns).astype(jnp.bfl...  215 us
    psum x2, blocking collectives, col_potential(): total = lax.psum(local_sum(score_of, targets, top, turns), 'row')  180 us
    gather x48, local copies, waits for them, and re-layouts, block_costs(): y_take = jnp.take(y_blocks, cols, axis=0)  133 us
    pmax x2, blocking collectives, row_potential(): top = lax.pmax(local_max(score_of, targets, shape_blocks, turns), 'col')  119 us
    all_gather x1, waiting for transfers between devices, body(): y_all = lax.all_gather(y_points, 'row', axis=0, tiled=True)  74.6 us
    all_gather x1, blocking collectives, body(): lax.all_gather(jnp.stack([log_b, g_init]), 'row', axis=1, tiled=True)  41.8 us
    all_gather x2, blocking collectives, _do_matrix(): back = lax.all_gather(work_x, axis_name=axis_key)  31 us
    gather x48, local copies, waits for them, and re-layouts, block_costs(): x_take = jnp.take(x_blocks, rows, axis=0)  27.8 us
  transfers between devices with their start and end apart: 2, of which 2 were waited for; matrix products, arithmetic and copies ran while one was open for 0% of the time, Pallas kernels for 0%

profile of v1, /device:TPU:1, one launch (start us, length us, event | category | flops | bytes accessed | tf_op | source)
XLA Modules:
  0.0 1061.1 jit_solution(5173893655891534176)
XLA Ops:
  10.2 19.6 %all-gather.2 = f32[16,1,256]{2,1,0:T(1,128)S(1)} all-gather(f32[1,1,256]{2,1,0:T(1,128)} %bitcast.185), channel_id=1, replica_groups=mesh['row'=32,'col'=16] {'col'}, dimensions={0}, use_global_device_ids=true | all-gather | bytes 17408 | tf_op jit(solution)/shard_map/all_gather | solution.py:70
  30.5 41.8 %all_gather.24 = f32[2,8192]{1,0:T(2,128)S(1)} all-gather(f32[2,256]{1,0:T(2,128)S(1)} %pad_maximum_fusion), channel_id=1, replica_groups=mesh['row'=32,'col'=16] {'row'}, dimensions={1}, use_global_device_ids=true | all-gather | bytes 67584 | tf_op jit(solution)/shard_map/all_gather | solution.py:72
  77.3 74.6 %all-gather.8.cloned.1.call-done = bf16[8192,256]{1,0:T(8,128)(2,1)} async-done(((bf16[256,256]{1,0:T(8,128)(2,1)}), bf16[8192,256]{1,0:T(8,128)(2,1)}) %all-gather.8.cloned.1.call-update) | async-done | bytes 4194320 | tf_op jit(solution)/shard_map/all_gather | solution.py:71
  151.9 3.3 fusion.112
  155.2 42.2 %while.104 = (s32[]{:T(128)}, f32[32,128]{1,0:T(8,128)S(1)}, s32[6,8]{1,0:T(8,128)S(1)}, pred[6,8]{1,0:T(8,128)(4,1)S(1)}, s32[6,8]{1,0:T(8,128)S(1)}, /*index=5...) while((s32[]{:T(128)}, f32[32,128]{1,0:T(8,128)S(1)}, ...), condition=%wide.region_3.8_spmd, body=%wide.region_0.7_spmd.sunk | while | flops 68558968 | bytes 3252905 | solution.py:29
  197.5 60.4 %pmax.28 = f32[32,128]{1,0:T(8,128)S(1)} all-reduce(f32[32,128]{1,0:T(8,128)S(1)} %get-tuple-element.1538), channel_id=1, replica_groups=mesh['row'=32,'col'=16] {'col'}, use_global_device_ids=true, to_apply=%region_4.9 | all-reduce | flops 4096 | bytes 32768 | tf_op jit(solution)/shard_map/pmax | solution.py:49
  257.9 45.7 %while.105 = (s32[]{:T(128)}, f32[32,128]{1,0:T(8,128)S(1)}, s32[6,8]{1,0:T(8,128)S(1)}, pred[6,8]{1,0:T(8,128)(4,1)S(1)}, s32[6,8]{1,0:T(8,128)S(1)}, /*index=5...) while((s32[]{:T(128)}, f32[32,128]{1,0:T(8,128)S(1)}, ...), condition=%wide.region_8.13_spmd, body=%wide.region_5.12_spmd.sunk | while | flops 68691064 | bytes 3273425 | solution.py:39
  303.6 15.5 %all-gather = f32[512,128]{1,0:T(8,128)S(1)} all-gather(f32[32,128]{1,0:T(8,128)S(1)} %get-tuple-element.1539), channel_id=2, replica_groups=mesh['row'=32,'col'=16] {'col'}, dimensions={0}, use_global_device_ids=true | all-gather | bytes 278528 | tf_op jit(solution)/shard_map/all_gather | solution.py:45
  319.2 42.5 %while.106 = (s32[]{:T(128)}, f32[64,128]{1,0:T(8,128)S(1)}, s32[6,8]{1,0:T(8,128)S(1)}, pred[6,8]{1,0:T(8,128)(4,1)S(1)}, s32[6,8]{1,0:T(8,128)S(1)}, /*index=5...) while((s32[]{:T(128)}, f32[64,128]{1,0:T(8,128)S(1)}, ...), condition=%wide.region_13.18_spmd, body=%wide.region_10.17_spmd.sunk | while | flops 68558968 | bytes 3252905 | solution.py:29
  322.2 2.8 gather_fusion.14
  329.3 2.8 gather_fusion.14
  343.4 2.8 gather_fusion.14
  350.5 2.8 gather_fusion.14
  361.7 105.9 %pmax.29 = bf16[64,128]{1,0:T(8,128)(2,1)S(1)} all-reduce(bf16[64,128]{1,0:T(8,128)(2,1)S(1)} %convert_element_type.12), channel_id=1, replica_groups=mesh['row'=32,'col'=16] {'row'}, use_global_device_ids=true, to_apply=%region_14.19 | all-reduce | flops 8192 | bytes 32768 | tf_op jit(solution)/shard_map/pmax | solution.py:55
  467.6 45.9 %while.107 = (s32[]{:T(128)}, f32[64,128]{1,0:T(8,128)S(1)}, s32[6,8]{1,0:T(8,128)S(1)}, pred[6,8]{1,0:T(8,128)(4,1)S(1)}, s32[6,8]{1,0:T(8,128)S(1)}, /*index=5...) while((s32[]{:T(128)}, f32[64,128]{1,0:T(8,128)S(1)}, ...), condition=%wide.region_18.23_spmd, body=%wide.region_15.22_spmd.sunk | while | flops 68691064 | bytes 3273425 | solution.py:39
  471.2 2.8 gather_fusion.20
  478.8 2.8 gather_fusion.20
  501.8 2.8 gather_fusion.20
  509.5 2.8 gather_fusion.20
  513.5 90.0 %psum.14 = f32[64,128]{1,0:T(8,128)S(1)} all-reduce(f32[64,128]{1,0:T(8,128)S(1)} %get-tuple-element.1541), channel_id=1, replica_groups=mesh['row'=32,'col'=16] {'row'}, use_global_device_ids=true, to_apply=%region_19.24 | all-reduce | flops 8192 | bytes 65536 | tf_op jit(solution)/shard_map/psum | solution.py:58
  603.6 42.2 %while.108 = (s32[]{:T(128)}, f32[32,128]{1,0:T(8,128)S(1)}, s32[6,8]{1,0:T(8,128)S(1)}, pred[6,8]{1,0:T(8,128)(4,1)S(1)}, s32[6,8]{1,0:T(8,128)S(1)}, /*index=5...) while((s32[]{:T(128)}, f32[32,128]{1,0:T(8,128)S(1)}, ...), condition=%wide.region_23.28_spmd, body=%wide.region_20.27_spmd.sunk | while | flops 68558968 | bytes 3252905 | solution.py:29
  645.8 58.2 %pmax.30 = f32[32,128]{1,0:T(8,128)S(1)} all-reduce(f32[32,128]{1,0:T(8,128)S(1)} %get-tuple-element.1542), channel_id=1, replica_groups=mesh['row'=32,'col'=16] {'col'}, use_global_device_ids=true, to_apply=%region_24.29 | all-reduce | flops 4096 | bytes 32768 | tf_op jit(solution)/shard_map/pmax | solution.py:49
  704.0 45.7 %while.109 = (s32[]{:T(128)}, f32[32,128]{1,0:T(8,128)S(1)}, s32[6,8]{1,0:T(8,128)S(1)}, pred[6,8]{1,0:T(8,128)(4,1)S(1)}, s32[6,8]{1,0:T(8,128)S(1)}, /*index=5...) while((s32[]{:T(128)}, f32[32,128]{1,0:T(8,128)S(1)}, ...), condition=%wide.region_28.33_spmd, body=%wide.region_25.32_spmd.sunk | while | flops 68691064 | bytes 3273425 | solution.py:39
  749.7 15.5 %all-gather.1 = f32[512,128]{1,0:T(8,128)S(1)} all-gather(f32[32,128]{1,0:T(8,128)S(1)} %get-tuple-element.1543), channel_id=3, replica_groups=mesh['row'=32,'col'=16] {'col'}, dimensions={0}, use_global_device_ids=true | all-gather | bytes 278528 | tf_op jit(solution)/shard_map/all_gather | solution.py:45
  765.3 42.5 %while.110 = (s32[]{:T(128)}, f32[64,128]{1,0:T(8,128)S(1)}, s32[6,8]{1,0:T(8,128)S(1)}, pred[6,8]{1,0:T(8,128)(4,1)S(1)}, s32[6,8]{1,0:T(8,128)S(1)}, /*index=5...) while((s32[]{:T(128)}, f32[64,128]{1,0:T(8,128)S(1)}, ...), condition=%wide.region_33.38_spmd, body=%wide.region_30.37_spmd.sunk | while | flops 68558968 | bytes 3252905 | solution.py:29
  768.3 2.8 gather_fusion.40
  775.4 2.8 gather_fusion.40
  782.5 2.8 gather_fusion.40
  789.6 2.8 gather_fusion.40
  807.8 109.2 %pmax.31 = bf16[64,128]{1,0:T(8,128)(2,1)S(1)} all-reduce(bf16[64,128]{1,0:T(8,128)(2,1)S(1)} %convert_element_type.14), channel_id=1, replica_groups=mesh['row'=32,'col'=16] {'row'}, use_global_device_ids=true, to_apply=%region_34.39 | all-reduce | flops 8192 | bytes 32768 | tf_op jit(solution)/shard_map/pmax | solution.py:55
  917.0 45.9 %while.111 = (s32[]{:T(128)}, f32[64,128]{1,0:T(8,128)S(1)}, s32[6,8]{1,0:T(8,128)S(1)}, pred[6,8]{1,0:T(8,128)(4,1)S(1)}, s32[6,8]{1,0:T(8,128)S(1)}, /*index=5...) while((s32[]{:T(128)}, f32[64,128]{1,0:T(8,128)S(1)}, ...), condition=%wide.region_38.43_spmd, body=%wide.region_35.42_spmd.sunk | while | flops 68691064 | bytes 3273425 | solution.py:39
  963.0 90.0 %psum.15 = f32[64,128]{1,0:T(8,128)S(1)} all-reduce(f32[64,128]{1,0:T(8,128)S(1)} %get-tuple-element.1545), channel_id=1, replica_groups=mesh['row'=32,'col'=16] {'row'}, use_global_device_ids=true, to_apply=%region_39.44 | all-reduce | flops 8192 | bytes 65536 | tf_op jit(solution)/shard_map/psum | solution.py:58
  (767 shorter events, 324.9 us)
Async XLA Ops:
  7.2 67.8 %all-gather.6.cloned.1.call-start = ((), (), s32[]{:S(2)}) async-start(), calls=%async_computation | async-start | bytes 2228224 | tf_op jit(solution)/shard_map/all_gather | solution.py:69
  7.9 144.0 %all-gather.8.cloned.1.call-start = ((), (), s32[]{:S(2)}) async-start(), calls=%async_computation.1 | async-start | bytes 4325376 | tf_op jit(solution)/shard_map/all_gather | solution.py:71
  75.0 80.3 %copy-start = (bf16[4096,256]{1,0:T(8,128)(2,1)S(1)}, bf16[4096,256]{1,0:T(8,128)(2,1)}, u32[]{:S(2)}) copy-start(bf16[4096,256]{1,0:T(8,128)(2,1)} %all-gather.6.cloned.1.call-done) | copy-start | bytes 6291460
Sparse Core Ops, SparseCore 0:
  11.0 63.9 all-gather.5
  77.1 74.7 all-gather.7
